TPU v7x, 32 devices: a whole 2x2x4 slice. The times are simulated.
32 devices in a mesh: grp: 2 (over x), lon: 16 (over z, y, core).
Axes of the slice: x: 2, y: 2, z: 4, core: 2. Of those that a mesh axis runs over, the one named last changes fastest.
Arguments:
- tracer_pert: float32 [4, 50, 32, 1024], P('grp', None, 'lon'), parts along dimension 0, may hold values from -60 to 60
- surface_pert: float32 [4, 32, 1024], P('grp', 'lon'), parts along dimension 0, may hold values from -60 to 60
- zonal_flow: float32 [50, 32, 1024], P(None, 'lon'), may hold values from -3.2 to 3.2
- merid_flow: float32 [50, 32, 1024], P(None, 'lon'), may hold values from -3.2 to 3.2
- bottom_level: int32 [32, 1024], P('lon'), may hold values from 0 to 50
Outputs:
- tracer_vec: float32 [4, 50, 32, 1024], P('grp', None, 'lon'), parts along dimension 0
- surface_vec: float32 [4, 32, 1024], P('grp', 'lon'), parts along dimension 0
- growth: float32 [6], P('grp'), parts along dimension 0
There are 2 independent parts, one for each index of `grp`. A program takes and returns all parts, laid end to end along the dimension named above; an argument that names none is the same for every part. Nothing has to cross between parts.
Inputs may be any that keep to these rules, and one draw needn't show every extreme that they name: `bottom_level`: 0 marks a land column, 50 a column wet to the bottom level.
All inputs are finite; a program needn't handle non-finite values.
Results may differ from a plain program's by a relative error of at most 0.0001.
Values sent between devices are 32-bit elements; how exact they have to be, the bound alone decides.
A program may use at most 64 MiB of HBM per device.

v0:
```python
import jax
import jax.numpy as jnp
from jax import lax
from jax.sharding import PartitionSpec as P

ITERS = 3
DIFFUSIVITY = 0.5
TIME_STEP = 0.2
SURFACE_COUPLING = 0.5
STERIC_GAIN = 2.0
EPSILON = 1e-06


def extended_2(block, sides, width):
    for axis, dim in sides:
        count = lax.axis_size(axis)
        forward = [(i, i + 1) for i in range(count - 1)]
        forward.append((count - 1, 0))
        backward = [(target, source) for source, target in forward]
        low = lax.ppermute(
            lax.slice_in_dim(block, block.shape[dim] - width, None, axis=dim), axis, forward
        )
        high = lax.ppermute(lax.slice_in_dim(block, 0, width, axis=dim), axis, backward)
        block = jnp.concatenate([low, block, high], axis=dim)
    return block


def tracer_update(tracer, zonal_flow, merid_flow, wet_cells):
    face_x = wet_cells[:, :-1] * wet_cells[:, 1:]
    flow_x = 0.5 * (zonal_flow[:, :-1] + zonal_flow[:, 1:])
    west_vals = tracer[:, :, :-1]
    east_vals = tracer[:, :, 1:]
    flux_x = face_x * (
        0.5 * flow_x * (west_vals + east_vals) - DIFFUSIVITY * (east_vals - west_vals)
    )
    div_x = flux_x[:, :, 1:] - flux_x[:, :, :-1]
    interior = tracer[:, :, 1:-1]
    wet_mid = wet_cells[:, 1:-1]
    merid_mid = merid_flow[:, 1:-1]
    face_y = wet_mid[..., :-1] * wet_mid[..., 1:]
    flow_y = 0.5 * (merid_mid[..., :-1] + merid_mid[..., 1:])
    flux_y = face_y * (
        0.5 * flow_y * (interior[..., :-1] + interior[..., 1:])
        - DIFFUSIVITY * (interior[..., 1:] - interior[..., :-1])
    )
    padded = jnp.pad(flux_y, ((0, 0), (0, 0), (0, 0), (1, 1)))
    div_y = padded[..., 1:] - padded[..., :-1]
    return interior - TIME_STEP * (div_x + div_y)


def surface_operator(extended, face_x, face_y):
    grad_x = face_x * (extended[:, 1:] - extended[:, :-1])
    lap_x = grad_x[:, 1:] - grad_x[:, :-1]
    center = extended[:, 1:-1]
    grad_y = face_y * (center[..., 1:] - center[..., :-1])
    padded = jnp.pad(grad_y, ((0, 0), (0, 0), (1, 1)))
    lap_y = padded[..., 1:] - padded[..., :-1]
    return center - SURFACE_COUPLING * (lap_x + lap_y)


def apply_operator(surface, face_x, face_y):
    extended = extended_2(surface, (("lon", 1),), 1)
    return surface_operator(extended, face_x, face_y)


def local_products(lhs_field, rhs_field):
    return jnp.sum(lhs_field * rhs_field, axis=(1, 2))


def residual_squares(residual):
    return lax.psum(local_products(residual, residual), "lon")


def on_device(tracer_pert, surface_pert, zonal_flow, merid_flow, bottom_level):
    vectors, levels_count, columns, lat_rows = tracer_pert.shape
    levels = jnp.arange(levels_count, dtype=jnp.float32)[:, None, None]
    depths = bottom_level.astype(jnp.float32)
    wet_cells = (levels < depths[None]).astype(jnp.float32)
    tracer = wet_cells[None] * tracer_pert
    lead_rows = vectors * levels_count
    stacked = jnp.concatenate(
        [
            tracer.reshape(lead_rows, columns, lat_rows),
            surface_pert,
            zonal_flow,
            merid_flow,
            depths[None],
        ],
        axis=0,
    )
    extended = extended_2(stacked, (("lon", 1),), 1)
    tracer_ext = extended[:lead_rows].reshape(vectors, levels_count, columns + 2, lat_rows)
    zonal_ext = extended[lead_rows + vectors : lead_rows + vectors + levels_count]
    merid_ext = extended[
        lead_rows + vectors + levels_count : lead_rows + vectors + 2 * levels_count
    ]
    depth_ext = extended[-1]
    wet_ext = (levels < depth_ext[None]).astype(jnp.float32)
    tracer = tracer_update(tracer_ext, zonal_ext, merid_ext, wet_ext)
    refreshed = extended_2(tracer, (("lon", 2),), 1)
    tracer = tracer_update(refreshed, zonal_ext, merid_ext, wet_ext)
    surface_rim = extended[lead_rows : lead_rows + vectors]
    depth_rim = extended[-1]
    land_free = (depth_rim > 0).astype(jnp.float32)
    height_ext = surface_rim * land_free[None]
    face_x = jnp.minimum(depth_rim[:-1], depth_rim[1:])
    depth_mid = depth_rim[1:-1]
    face_y = jnp.minimum(depth_mid[:, :-1], depth_mid[:, 1:])
    height = height_ext[:, 1:-1]
    forcing = height + STERIC_GAIN * jnp.sum(tracer, axis=1) / levels_count
    residual = forcing - surface_operator(height_ext, face_x, face_y)
    solution = height
    direction = residual
    norm_now = residual_squares(residual)
    for iteration in range(ITERS):
        image_vec = apply_operator(direction, face_x, face_y)
        step_size = norm_now / lax.psum(local_products(direction, image_vec), "lon")
        solution = solution + step_size[:, None, None] * direction
        residual = residual - step_size[:, None, None] * image_vec
        if iteration + 1 < ITERS:
            norm_next = residual_squares(residual)
            direction = residual + (norm_next / norm_now)[:, None, None] * direction
            norm_now = norm_next
    cell_count = (levels_count + 1) * columns * lat_rows * lax.axis_size("lon")

    def local_inner(tracer_a, surface_a, tracer_b, surface_b):
        return (jnp.sum(tracer_a * tracer_b) + jnp.sum(surface_a * surface_b)) / cell_count

    first_tracer, second_tracer = (tracer[0], tracer[1])
    first_surface, second_surface = (solution[0], solution[1])
    gram_one, gram_mix, gram_two = lax.psum(
        (
            local_inner(first_tracer, first_surface, first_tracer, first_surface),
            local_inner(second_tracer, second_surface, first_tracer, first_surface),
            local_inner(second_tracer, second_surface, second_tracer, second_surface),
        ),
        "lon",
    )
    scale_one = jnp.sqrt(gram_one + EPSILON)
    cross = gram_mix / scale_one
    unit_tracer = first_tracer / scale_one
    unit_surface = first_surface / scale_one
    rest_tracer = second_tracer - cross * unit_tracer
    rest_surface = second_surface - cross * unit_surface
    rest_norm = gram_two - 2.0 * cross * cross + cross * cross * gram_one / (gram_one + EPSILON)
    scale_two = jnp.sqrt(rest_norm + EPSILON)
    tracer_vec = jnp.stack([unit_tracer, rest_tracer / scale_two])
    surface_vec = jnp.stack([unit_surface, rest_surface / scale_two])
    growth = jnp.stack([scale_one, cross, scale_two])
    return (tracer_vec, surface_vec, growth)


def solution(mesh):
    placed = (
        P("grp", None, "lon", None),
        P("grp", "lon", None),
        P(None, "lon", None),
        P(None, "lon", None),
        P("lon", None),
    )
    return jax.shard_map(
        on_device,
        mesh=mesh,
        in_specs=placed,
        out_specs=(P("grp", None, "lon", None), P("grp", "lon", None), P("grp")),
        check_vma=False,
    )
```

profile of v0, /device:TPU:0, one launch (start us, length us, event | category | flops | bytes accessed | tf_op | source)
XLA Modules:
  0.0 270.8 jit_solution(4647945465952432828)
XLA Ops:
  0.6 0.7 convert_element_type.23
  1.3 0.2 compare_convert_fusion
  1.5 1.6 broadcast_multiply_fusion
  3.3 0.8 copy-done
  4.2 1.3 fusion.35
  5.5 0.2 copy.20
  5.6 5.5 %collective-permute-start.1 = (f32[203,1,1024]{2,0,1:T(8,128)S(1)}, f32[203,1,1024]{2,0,1:T(8,128)S(1)}, u32[]{:S(2)}, u32[]{:S(2)}) collective-permute-start(f32[203,1,1024]{2,0,1:T(8,128)S(1)} %copy.20), channel_id=1, source_target_pairs={{1,0},{2,1},{3,2},{4,3},{5,4},{6,5},{7,6},{8,7},{9,8},{10,9},{11,1... | collective-permute-start | bytes 2494472 | tf_op jit(solution)/shard_map/ppermute | solution.py:23
  11.1 0.2 copy.19
  11.3 0.2 collective-permute-start
  11.5 0.1 slice_minimum_fusion
  11.6 0.5 add_multiply_fusion
  12.1 9.2 %collective-permute-done.1 = f32[203,1,1024]{2,0,1:T(8,128)S(1)} collective-permute-done((f32[203,1,1024]{2,0,1:T(8,128)S(1)}, f32[203,1,1024]{2,0,1:T(8,128)S(1)}, u32[]{:S(2)}, u32[]{:S(2)}) %collective-permute-start.1) | collective-permute-done | bytes 831520 | tf_op jit(solution)/shard_map/ppermute | solution.py:23
  21.4 0.9 copy.22
  22.2 4.2 %collective-permute-done = f32[203,1,1024]{2,0,1:T(8,128)S(1)} collective-permute-done((f32[203,1,1024]{2,0,1:T(8,128)S(1)}, f32[203,1,1024]{2,0,1:T(8,128)S(1)}, u32[]{:S(2)}, u32[]{:S(2)}) %collective-permute-start) | collective-permute-done | bytes 831520 | tf_op jit(solution)/shard_map/ppermute | solution.py:20
  26.4 0.9 copy.21
  27.4 0.2 fusion.7
  27.6 0.5 slice_multiply_fusion.1
  28.1 0.9 fusion.6
  29.0 2.6 pad_maximum_fusion
  31.6 0.1 slice.349
  31.7 1.5 subtract_multiply_fusion.3
  33.2 0.9 subtract_multiply_fusion.1
  34.1 1.5 fusion.5
  35.6 0.6 fusion.36
  36.3 2.8 %collective-permute-start.2 = (f32[2,50,1,1024]{3,2,1,0:T(1,128)S(1)}, f32[2,50,1,1024]{3,2,1,0:T(1,128)S(1)}, u32[]{:S(2)}, u32[]{:S(2)}) collective-permute-start(f32[2,50,1,1024]{3,2,1,0:T(1,128)S(1)} %get-tuple-element.36), channel_id=1, source_target_pairs={{0,1},{1,2},{2,3},{3,4},{4,5},{5,6},{6,7},{7,8},{8,9},{9,10},{10,1... | collective-permute-start | bytes 1228808 | tf_op jit(solution)/shard_map/ppermute | solution.py:20
  39.0 1.7 collective-permute-start.3
  40.8 0.1 fusion.24
  40.9 1.1 subtract_multiply_fusion.2
  42.0 4.5 %collective-permute-done.2 = f32[2,50,1,1024]{3,2,1,0:T(1,128)S(1)} collective-permute-done((f32[2,50,1,1024]{3,2,1,0:T(1,128)S(1)}, f32[2,50,1,1024]{3,2,1,0:T(1,128)S(1)}, u32[]{:S(2)}, u32[]{:S(2)}) %collective-permute-start.2) | collective-permute-done | bytes 409632 | tf_op jit(solution)/shard_map/ppermute | solution.py:20
  46.5 1.7 subtract_multiply_fusion
  48.3 1.5 fusion.33
  49.8 0.1 fusion.28
  49.9 4.2 %collective-permute-start.5 = (f32[2,1,1024]{2,1,0:T(1,128)S(1)}, f32[2,1,1024]{2,1,0:T(1,128)S(1)}, u32[]{:S(2)}, u32[]{:S(2)}) collective-permute-start(f32[2,1,1024]{2,1,0:T(1,128)S(1)} %get-tuple-element.42), channel_id=1, source_target_pairs={{0,1},{1,2},{2,3},{3,4},{4,5},{5,6},{6,7},{7,8},{8,9},{9,10},{10,1... | collective-permute-start | bytes 24584 | tf_op jit(solution)/shard_map/ppermute | solution.py:20
  54.1 0.4 collective-permute-start.4
  54.5 0.1 fusion.20
  54.6 1.2 collective-permute-done.5
  55.7 0.5 collective-permute-done.4
  56.3 0.2 multiply_reduce_fusion.6
  56.4 33.5 %all-reduce.7 = (f32[2]{0:T(128)S(1)}, f32[2]{0:T(128)S(1)}) all-reduce(f32[2]{0:T(128)S(1)} %get-tuple-element.13, f32[2]{0:T(128)S(1)} %get-tuple-element.12), channel_id=1, replica_groups=mesh['grp'=2,'lon'=16] {'lon'}, use_global_device_ids=true, to_apply=%region_3.4 | all-reduce | flops 4 | bytes 32 | tf_op jit(solution)/shard_map/psum | solution.py:71
  89.9 0.2 multiply_reduce_fusion.5
  90.1 29.5 %psum.65 = f32[2]{0:T(128)S(1)} all-reduce(f32[2]{0:T(128)S(1)} %get-tuple-element.27), channel_id=1, replica_groups=mesh['grp'=2,'lon'=16] {'lon'}, use_global_device_ids=true, to_apply=%region_7.8 | all-reduce | flops 2 | bytes 16 | tf_op jit(solution)/shard_map/psum | solution.py:71
  119.6 0.1 multiply_add_fusion.2
  119.7 0.1 collective-permute-start.7
  119.8 4.4 %collective-permute-start.6 = (f32[2,1,1024]{2,1,0:T(1,128)S(1)}, f32[2,1,1024]{2,1,0:T(1,128)S(1)}, u32[]{:S(2)}, u32[]{:S(2)}) collective-permute-start(f32[2,1,1024]{2,1,0:T(1,128)S(1)} %get-tuple-element.41), channel_id=1, source_target_pairs={{1,0},{2,1},{3,2},{4,3},{5,4},{6,5},{7,6},{8,7},{9,8},{10,9},{11,1... | collective-permute-start | bytes 24584 | tf_op jit(solution)/shard_map/ppermute | solution.py:23
  124.2 0.1 fusion.16
  124.3 1.2 collective-permute-done.7
  125.6 0.2 multiply_reduce_fusion.4
  125.8 33.9 %psum.66 = f32[2]{0:T(128)S(1)} all-reduce(f32[2]{0:T(128)S(1)} %get-tuple-element.25), channel_id=1, replica_groups=mesh['grp'=2,'lon'=16] {'lon'}, use_global_device_ids=true, to_apply=%region_9.10 | all-reduce | flops 2 | bytes 16 | tf_op jit(solution)/shard_map/psum | solution.py:117
  159.7 0.2 multiply_reduce_fusion.3
  159.9 29.5 %psum.67 = f32[2]{0:T(128)S(1)} all-reduce(f32[2]{0:T(128)S(1)} %get-tuple-element.23), channel_id=1, replica_groups=mesh['grp'=2,'lon'=16] {'lon'}, use_global_device_ids=true, to_apply=%region_11.12 | all-reduce | flops 2 | bytes 16 | tf_op jit(solution)/shard_map/psum | solution.py:71
  189.3 0.1 multiply_add_fusion.1
  189.5 4.4 %collective-permute-start.8 = (f32[2,1,1024]{2,1,0:T(1,128)S(1)}, f32[2,1,1024]{2,1,0:T(1,128)S(1)}, u32[]{:S(2)}, u32[]{:S(2)}) collective-permute-start(f32[2,1,1024]{2,1,0:T(1,128)S(1)} %get-tuple-element.39), channel_id=1, source_target_pairs={{1,0},{2,1},{3,2},{4,3},{5,4},{6,5},{7,6},{8,7},{9,8},{10,9},{11,1... | collective-permute-start | bytes 24584 | tf_op jit(solution)/shard_map/ppermute | solution.py:23
  193.9 0.1 fusion.13
  194.0 1.2 collective-permute-done.9
  195.3 0.2 fusion.12
  195.5 1.2 multiply_reduce_fusion.1
  196.8 33.9 %psum.68 = f32[2]{0:T(128)S(1)} all-reduce(f32[2]{0:T(128)S(1)} %fusion.12), channel_id=1, replica_groups=mesh['grp'=2,'lon'=16] {'lon'}, use_global_device_ids=true, to_apply=%region_13.14 | all-reduce | flops 2 | bytes 16 | tf_op jit(solution)/shard_map/psum | solution.py:117
  230.6 0.1 multiply_add_fusion
  230.7 0.7 multiply_reduce_fusion.9
  235.2 30.0 %all-reduce.6 = (f32[]{:T(128)}, f32[]{:T(128)}, f32[]{:T(128)}) all-reduce(f32[]{:T(128)S(6)} %div.73, f32[]{:T(128)S(6)} %div.78, f32[]{:T(128)S(6)} %div.76), channel_id=1, replica_groups=mesh['grp'=2,'lon'=16] {'lon'}, use_global_device_ids=true, to_apply=%region_15.16 | all-reduce | flops 3 | bytes 24 | tf_op jit(solution)/shard_map/psum | solution.py:131
  268.0 0.3 subtract_divide_fusion
  268.3 0.6 pad_maximum_fusion.7
  268.9 1.3 pad_maximum_fusion.3
  270.2 0.6 pad_maximum_fusion.8
  (32 shorter events, 0.6 us)
Async XLA Ops:
  1.5 1.7 copy-start.3
  1.5 1.7 copy-start.1
  3.1 1.0 copy-start
  3.1 1.1 copy-start.2
  5.6 15.7 %collective-permute-start.1 = (f32[203,1,1024]{2,0,1:T(8,128)S(1)}, f32[203,1,1024]{2,0,1:T(8,128)S(1)}, u32[]{:S(2)}, u32[]{:S(2)}) collective-permute-start(f32[203,1,1024]{2,0,1:T(8,128)S(1)} %copy.20), channel_id=1, source_target_pairs={{1,0},{2,1},{3,2},{4,3},{5,4},{6,5},{7,6},{8,7},{9,8},{10,9},{11,1... | collective-permute-start | bytes 2494472 | tf_op jit(solution)/shard_map/ppermute | solution.py:23
  11.3 15.1 %collective-permute-start = (f32[203,1,1024]{2,0,1:T(8,128)S(1)}, f32[203,1,1024]{2,0,1:T(8,128)S(1)}, u32[]{:S(2)}, u32[]{:S(2)}) collective-permute-start(f32[203,1,1024]{2,0,1:T(8,128)S(1)} %copy.19), channel_id=1, source_target_pairs={{0,1},{1,2},{2,3},{3,4},{4,5},{5,6},{6,7},{7,8},{8,9},{9,10},{10,1... | collective-permute-start | bytes 2494472 | tf_op jit(solution)/shard_map/ppermute | solution.py:20
  36.3 10.2 %collective-permute-start.2 = (f32[2,50,1,1024]{3,2,1,0:T(1,128)S(1)}, f32[2,50,1,1024]{3,2,1,0:T(1,128)S(1)}, u32[]{:S(2)}, u32[]{:S(2)}) collective-permute-start(f32[2,50,1,1024]{3,2,1,0:T(1,128)S(1)} %get-tuple-element.36), channel_id=1, source_target_pairs={{0,1},{1,2},{2,3},{3,4},{4,5},{5,6},{6,7},{7,8},{8,9},{9,10},{10,1... | collective-permute-start | bytes 1228808 | tf_op jit(solution)/shard_map/ppermute | solution.py:20
  39.0 7.5 %collective-permute-start.3 = (f32[2,50,1,1024]{3,2,1,0:T(1,128)S(1)}, f32[2,50,1,1024]{3,2,1,0:T(1,128)S(1)}, u32[]{:S(2)}, u32[]{:S(2)}) collective-permute-start(f32[2,50,1,1024]{3,2,1,0:T(1,128)S(1)} %get-tuple-element.37), channel_id=1, source_target_pairs={{1,0},{2,1},{3,2},{4,3},{5,4},{6,5},{7,6},{8,7},{9,8},{10,9},{11,1... | collective-permute-start | bytes 1228808 | tf_op jit(solution)/shard_map/ppermute | solution.py:23
  49.9 5.8 %collective-permute-start.5 = (f32[2,1,1024]{2,1,0:T(1,128)S(1)}, f32[2,1,1024]{2,1,0:T(1,128)S(1)}, u32[]{:S(2)}, u32[]{:S(2)}) collective-permute-start(f32[2,1,1024]{2,1,0:T(1,128)S(1)} %get-tuple-element.42), channel_id=1, source_target_pairs={{0,1},{1,2},{2,3},{3,4},{4,5},{5,6},{6,7},{7,8},{8,9},{9,10},{10,1... | collective-permute-start | bytes 24584 | tf_op jit(solution)/shard_map/ppermute | solution.py:20
  54.1 2.1 collective-permute-start.4
  119.7 5.8 %collective-permute-start.7 = (f32[2,1,1024]{2,1,0:T(1,128)S(1)}, f32[2,1,1024]{2,1,0:T(1,128)S(1)}, u32[]{:S(2)}, u32[]{:S(2)}) collective-permute-start(f32[2,1,1024]{2,1,0:T(1,128)S(1)} %get-tuple-element.40), channel_id=1, source_target_pairs={{0,1},{1,2},{2,3},{3,4},{4,5},{5,6},{6,7},{7,8},{8,9},{9,10},{10,1... | collective-permute-start | bytes 24584 | tf_op jit(solution)/shard_map/ppermute | solution.py:20
  119.8 5.8 %collective-permute-start.6 = (f32[2,1,1024]{2,1,0:T(1,128)S(1)}, f32[2,1,1024]{2,1,0:T(1,128)S(1)}, u32[]{:S(2)}, u32[]{:S(2)}) collective-permute-start(f32[2,1,1024]{2,1,0:T(1,128)S(1)} %get-tuple-element.41), channel_id=1, source_target_pairs={{1,0},{2,1},{3,2},{4,3},{5,4},{6,5},{7,6},{8,7},{9,8},{10,9},{11,1... | collective-permute-start | bytes 24584 | tf_op jit(solution)/shard_map/ppermute | solution.py:23
  189.4 5.8 %collective-permute-start.9 = (f32[2,1,1024]{2,1,0:T(1,128)S(1)}, f32[2,1,1024]{2,1,0:T(1,128)S(1)}, u32[]{:S(2)}, u32[]{:S(2)}) collective-permute-start(f32[2,1,1024]{2,1,0:T(1,128)S(1)} %get-tuple-element.38), channel_id=1, source_target_pairs={{0,1},{1,2},{2,3},{3,4},{4,5},{5,6},{6,7},{7,8},{8,9},{9,10},{10,1... | collective-permute-start | bytes 24584 | tf_op jit(solution)/shard_map/ppermute | solution.py:20
  189.5 5.8 %collective-permute-start.8 = (f32[2,1,1024]{2,1,0:T(1,128)S(1)}, f32[2,1,1024]{2,1,0:T(1,128)S(1)}, u32[]{:S(2)}, u32[]{:S(2)}) collective-permute-start(f32[2,1,1024]{2,1,0:T(1,128)S(1)} %get-tuple-element.39), channel_id=1, source_target_pairs={{1,0},{2,1},{3,2},{4,3},{5,4},{6,5},{7,6},{8,7},{9,8},{10,9},{11,1... | collective-permute-start | bytes 24584 | tf_op jit(solution)/shard_map/ppermute | solution.py:23
where the time goes:
time: 271 us
  blocking collectives  190 us (70%)
  starting transfers between devices  23.8 us (9%)
  waiting for transfers between devices  22.2 us (8%)
  other arithmetic  21.9 us (8%)
  between operations  7.55 us (3%)
  local copies, waits for them, and re-layouts  5.13 us (2%)
    psum x3, blocking collectives, residual_squares(): return lax.psum(local_products(residual, residual), 'lon')  92.5 us
    psum x2, blocking collectives, on_device(): step_size = norm_now / lax.psum(local_products(direction, image_vec), 'lon')  67.8 us
    psum x1, blocking collectives, on_device(): lax.psum((local_inner(first_tracer, first_surface, first_tracer, first_su...  30 us
    ppermute x5, starting transfers between devices, extended_2(): lax.ppermute(lax.slice_in_dim(block, 0, width, axis=dim), axis, backward)  16.5 us
    ppermute x5, waiting for transfers between devices, extended_2(): lax.ppermute(lax.slice_in_dim(block, block.shape[dim] - width, None, axis...  12.4 us
    ppermute x5, waiting for transfers between devices, extended_2(): lax.ppermute(lax.slice_in_dim(block, 0, width, axis=dim), axis, backward)  9.78 us
    ppermute x5, starting transfers between devices, extended_2(): lax.ppermute(lax.slice_in_dim(block, block.shape[dim] - width, None, axis...  7.28 us
  transfers between devices with their start and end apart: 10, of which 7 were waited for; matrix products, arithmetic and copies ran while one was open for 1% of the time, Pallas kernels for 0%

commit v1 on v0

--- a/solution.py
+++ b/solution.py
@@ -9,6 +9,11 @@
 SURFACE_COUPLING = 0.5
 STERIC_GAIN = 2.0
 EPSILON = 1e-06
+
+
+def cards_assign(sample, across):
+    carry_in = jax.lax.all_gather(sample, across)
+    return jnp.sum(carry_in, axis=0)
 
 
 def extended_2(block, sides, width):
@@ -114,7 +119,7 @@
     norm_now = residual_squares(residual)
     for iteration in range(ITERS):
         image_vec = apply_operator(direction, face_x, face_y)
-        step_size = norm_now / lax.psum(local_products(direction, image_vec), "lon")
+        step_size = norm_now / cards_assign(local_products(direction, image_vec), "lon")
         solution = solution + step_size[:, None, None] * direction
         residual = residual - step_size[:, None, None] * image_vec
         if iteration + 1 < ITERS:

time: 271 us -> 273 us (level)
  local copies, waits for them, and re-layouts: 5.13 us -> 9.85 us
  waiting for transfers between devices: 22.2 us -> 18.6 us
    unnamed x0 -> x2, blocking collectives: none -> 67.8 us
    psum x2 -> x0, blocking collectives: 67.8 us -> none  [on_device(): step_size = norm_now / lax.psum(local_products(direction, image_vec), 'lon')]
  transfers between devices with their start and end apart: 10 -> 10, of which waited for: 7 -> 6; matrix products, arithmetic and copies ran while one was open for 1% -> 2% of each run, Pallas kernels for 0% -> 0%
where the time goes in v1:
time: 273 us
  blocking collectives  191 us (70%)
  starting transfers between devices  23.6 us (9%)
  other arithmetic  22 us (8%)
  waiting for transfers between devices  18.6 us (7%)
  local copies, waits for them, and re-layouts  9.85 us (4%)
  between operations  8.22 us (3%)
    psum x3, blocking collectives, residual_squares(): return lax.psum(local_products(residual, residual), 'lon')  92.8 us
    unnamed x2, blocking collectives  67.8 us
    psum x1, blocking collectives, on_device(): lax.psum((local_inner(first_tracer, first_surface, first_tracer, first_su...  30 us
    ppermute x5, starting transfers between devices, extended_2(): lax.ppermute(lax.slice_in_dim(block, 0, width, axis=dim), axis, backward)  16.3 us
    ppermute x5, waiting for transfers between devices, extended_2(): lax.ppermute(lax.slice_in_dim(block, block.shape[dim] - width, None, axis...  11.1 us
    ppermute x5, waiting for transfers between devices, extended_2(): lax.ppermute(lax.slice_in_dim(block, 0, width, axis=dim), axis, backward)  7.49 us
    ppermute x5, starting transfers between devices, extended_2(): lax.ppermute(lax.slice_in_dim(block, block.shape[dim] - width, None, axis...  7.3 us
  transfers between devices with their start and end apart: 10, of which 6 were waited for; matrix products, arithmetic and copies ran while one was open for 2% of the time, Pallas kernels for 0%

profile of v1, /device:TPU:0, one launch (start us, length us, event | category | flops | bytes accessed | tf_op | source)
XLA Modules:
  0.0 272.8 jit_solution(280202211000675928)
XLA Ops:
  0.6 0.7 convert_element_type.23
  1.3 0.2 compare_convert_fusion
  1.5 1.6 broadcast_multiply_fusion
  3.3 0.8 copy-done
  4.2 1.3 fusion.35
  5.5 0.2 copy.20
  5.6 5.5 %collective-permute-start.1 = (f32[203,1,1024]{2,0,1:T(8,128)S(1)}, f32[203,1,1024]{2,0,1:T(8,128)}, u32[]{:S(2)}, u32[]{:S(2)}) collective-permute-start(f32[203,1,1024]{2,0,1:T(8,128)S(1)} %copy.20), channel_id=1, source_target_pairs={{1,0},{2,1},{3,2},{4,3},{5,4},{6,5},{7,6},{8,7},{9,8},{10,9},{11,1... | collective-permute-start | bytes 2494472 | tf_op jit(solution)/shard_map/ppermute | solution.py:28
  11.2 1.1 copy.19
  12.2 0.6 dynamic-slice
  13.5 0.5 add_multiply_fusion
  14.0 7.3 %collective-permute-done.1 = f32[203,1,1024]{2,0,1:T(8,128)} collective-permute-done((f32[203,1,1024]{2,0,1:T(8,128)S(1)}, f32[203,1,1024]{2,0,1:T(8,128)}, u32[]{:S(2)}, u32[]{:S(2)}) %collective-permute-start.1) | collective-permute-done | bytes 831520 | tf_op jit(solution)/shard_map/ppermute | solution.py:28
  21.4 2.0 copy.22
  23.4 4.1 %collective-permute-done = f32[203,1,1024]{2,0,1:T(8,128)} collective-permute-done((f32[203,1,1024]{2,0,1:T(8,128)}, f32[203,1,1024]{2,0,1:T(8,128)}, u32[]{:S(2)}, u32[]{:S(2)}) %collective-permute-start) | collective-permute-done | bytes 831520 | tf_op jit(solution)/shard_map/ppermute | solution.py:25
  27.5 2.0 copy.21
  29.5 0.2 fusion.7
  29.7 0.5 slice_multiply_fusion.1
  30.2 0.9 fusion.6
  31.1 2.6 pad_maximum_fusion
  33.7 0.1 slice.349
  33.9 1.5 subtract_multiply_fusion.3
  35.4 0.9 subtract_multiply_fusion.1
  36.3 1.5 fusion.5
  37.8 0.6 fusion.36
  38.4 3.0 %collective-permute-start.2 = (f32[2,50,1,1024]{3,2,1,0:T(1,128)S(1)}, f32[2,50,1,1024]{3,2,1,0:T(1,128)S(1)}, u32[]{:S(2)}, u32[]{:S(2)}) collective-permute-start(f32[2,50,1,1024]{3,2,1,0:T(1,128)S(1)} %get-tuple-element.36), channel_id=1, source_target_pairs={{0,1},{1,2},{2,3},{3,4},{4,5},{5,6},{6,7},{7,8},{8,9},{9,10},{10,1... | collective-permute-start | bytes 1228808 | tf_op jit(solution)/shard_map/ppermute | solution.py:25
  41.5 1.5 collective-permute-start.3
  43.0 0.1 fusion.24
  43.0 1.1 subtract_multiply_fusion.2
  44.1 4.5 %collective-permute-done.2 = f32[2,50,1,1024]{3,2,1,0:T(1,128)S(1)} collective-permute-done((f32[2,50,1,1024]{3,2,1,0:T(1,128)S(1)}, f32[2,50,1,1024]{3,2,1,0:T(1,128)S(1)}, u32[]{:S(2)}, u32[]{:S(2)}) %collective-permute-start.2) | collective-permute-done | bytes 409632 | tf_op jit(solution)/shard_map/ppermute | solution.py:25
  48.7 1.7 subtract_multiply_fusion
  50.4 1.5 fusion.33
  52.0 0.1 fusion.28
  52.1 0.1 fusion.20
  52.2 4.2 %collective-permute-start.5 = (f32[2,1,1024]{2,1,0:T(1,128)S(1)}, f32[2,1,1024]{2,1,0:T(1,128)S(1)}, u32[]{:S(2)}, u32[]{:S(2)}) collective-permute-start(f32[2,1,1024]{2,1,0:T(1,128)S(1)} %get-tuple-element.42), channel_id=1, source_target_pairs={{0,1},{1,2},{2,3},{3,4},{4,5},{5,6},{6,7},{7,8},{8,9},{9,10},{10,1... | collective-permute-start | bytes 24584 | tf_op jit(solution)/shard_map/ppermute | solution.py:25
  56.3 0.4 collective-permute-start.4
  56.7 1.2 multiply_reduce_fusion.1
  58.0 0.1 collective-permute-done.4
  58.1 0.2 multiply_reduce_fusion.6
  58.3 0.2 dynamic-update-slice
  58.6 33.9 %all-reduce.10 = (f32[2]{0:T(128)S(1)}, f32[32]{0:T(128)S(1)}) all-reduce(f32[2]{0:T(128)S(1)} %get-tuple-element.13, f32[32]{0:T(128)S(1)} %dynamic-update-slice), channel_id=1, replica_groups=mesh['grp'=2,'lon'=16] {'lon'}, use_global_device_ids=true, to_apply=%region_3.4 | all-reduce | flops 34 | bytes 272 | tf_op jit(solution)/shard_map/psum | solution.py:76
  92.4 0.1 reshape.40
  92.6 0.2 multiply_reduce_fusion.5
  92.7 29.5 %psum.43 = f32[2]{0:T(128)S(1)} all-reduce(f32[2]{0:T(128)S(1)} %get-tuple-element.27), channel_id=1, replica_groups=mesh['grp'=2,'lon'=16] {'lon'}, use_global_device_ids=true, to_apply=%region_7.8 | all-reduce | flops 2 | bytes 16 | tf_op jit(solution)/shard_map/psum | solution.py:76
  122.4 4.4 %collective-permute-start.6 = (f32[2,1,1024]{2,1,0:T(1,128)S(1)}, f32[2,1,1024]{2,1,0:T(1,128)S(1)}, u32[]{:S(2)}, u32[]{:S(2)}) collective-permute-start(f32[2,1,1024]{2,1,0:T(1,128)S(1)} %get-tuple-element.41), channel_id=1, source_target_pairs={{1,0},{2,1},{3,2},{4,3},{5,4},{6,5},{7,6},{8,7},{9,8},{10,9},{11,1... | collective-permute-start | bytes 24584 | tf_op jit(solution)/shard_map/ppermute | solution.py:28
  126.8 0.1 fusion.16
  126.9 1.2 collective-permute-done.7
  128.2 0.2 multiply_reduce_fusion.4
  128.4 0.2 dynamic-update-slice.1
  128.6 33.9 %all-reduce.7 = f32[32]{0:T(128)S(1)} all-reduce(f32[32]{0:T(128)S(1)} %dynamic-update-slice.1), channel_id=3, replica_groups=mesh['grp'=2,'lon'=16] {'lon'}, use_global_device_ids=true, to_apply=%add.7 | all-reduce | flops 32 | bytes 256
  162.5 0.1 reshape.41
  162.6 0.2 multiply_reduce_fusion.3
  162.8 29.5 %psum.44 = f32[2]{0:T(128)S(1)} all-reduce(f32[2]{0:T(128)S(1)} %get-tuple-element.23), channel_id=1, replica_groups=mesh['grp'=2,'lon'=16] {'lon'}, use_global_device_ids=true, to_apply=%region_11.12 | all-reduce | flops 2 | bytes 16 | tf_op jit(solution)/shard_map/psum | solution.py:76
  192.4 4.4 %collective-permute-start.8 = (f32[2,1,1024]{2,1,0:T(1,128)S(1)}, f32[2,1,1024]{2,1,0:T(1,128)S(1)}, u32[]{:S(2)}, u32[]{:S(2)}) collective-permute-start(f32[2,1,1024]{2,1,0:T(1,128)S(1)} %get-tuple-element.39), channel_id=1, source_target_pairs={{1,0},{2,1},{3,2},{4,3},{5,4},{6,5},{7,6},{8,7},{9,8},{10,9},{11,1... | collective-permute-start | bytes 24584 | tf_op jit(solution)/shard_map/ppermute | solution.py:28
  197.0 1.2 collective-permute-done.9
  198.3 0.2 fusion.12
  198.5 0.2 dynamic-update-slice.2
  198.7 33.9 %all-reduce.8 = f32[32]{0:T(128)S(1)} all-reduce(f32[32]{0:T(128)S(1)} %dynamic-update-slice.2), channel_id=4, replica_groups=mesh['grp'=2,'lon'=16] {'lon'}, use_global_device_ids=true, to_apply=%add.8 | all-reduce | flops 32 | bytes 256
  232.5 0.1 reshape.42
  232.7 0.1 multiply_add_fusion
  232.8 0.7 multiply_reduce_fusion.9
  237.3 30.0 %all-reduce.9 = (f32[]{:T(128)}, f32[]{:T(128)}, f32[]{:T(128)}) all-reduce(f32[]{:T(128)S(6)} %div.73, f32[]{:T(128)S(6)} %div.78, f32[]{:T(128)S(6)} %div.76), channel_id=1, replica_groups=mesh['grp'=2,'lon'=16] {'lon'}, use_global_device_ids=true, to_apply=%region_15.16 | all-reduce | flops 3 | bytes 24 | tf_op jit(solution)/shard_map/psum | solution.py:136
  270.0 0.3 subtract_divide_fusion
  270.3 0.6 pad_maximum_fusion.7
  270.9 1.3 pad_maximum_fusion.3
  272.3 0.6 pad_maximum_fusion.8
  (47 shorter events, 1.1 us)
Async XLA Ops:
  1.5 1.7 copy-start.3
  1.5 1.7 copy-start.1
  3.1 1.0 copy-start
  3.1 1.1 copy-start.2
  5.5 6.8 %copy-start.4 = (u32[32]{0:T(128)S(1)}, u32[32]{0:T(128)}, u32[]{:S(2)}) copy-start(u32[32]{0:T(128)} %constant.49) | copy-start | bytes 388
  5.6 15.7 %collective-permute-start.1 = (f32[203,1,1024]{2,0,1:T(8,128)S(1)}, f32[203,1,1024]{2,0,1:T(8,128)}, u32[]{:S(2)}, u32[]{:S(2)}) collective-permute-start(f32[203,1,1024]{2,0,1:T(8,128)S(1)} %copy.20), channel_id=1, source_target_pairs={{1,0},{2,1},{3,2},{4,3},{5,4},{6,5},{7,6},{8,7},{9,8},{10,9},{11,1... | collective-permute-start | bytes 2494472 | tf_op jit(solution)/shard_map/ppermute | solution.py:28
  12.2 15.2 %collective-permute-start = (f32[203,1,1024]{2,0,1:T(8,128)}, f32[203,1,1024]{2,0,1:T(8,128)}, u32[]{:S(2)}, u32[]{:S(2)}) collective-permute-start(f32[203,1,1024]{2,0,1:T(8,128)} %copy.19), channel_id=1, source_target_pairs={{0,1},{1,2},{2,3},{3,4},{4,5},{5,6},{6,7},{7,8},{8,9},{9,10},{10,1... | collective-permute-start | bytes 2494472 | tf_op jit(solution)/shard_map/ppermute | solution.py:25
  38.4 10.2 %collective-permute-start.2 = (f32[2,50,1,1024]{3,2,1,0:T(1,128)S(1)}, f32[2,50,1,1024]{3,2,1,0:T(1,128)S(1)}, u32[]{:S(2)}, u32[]{:S(2)}) collective-permute-start(f32[2,50,1,1024]{3,2,1,0:T(1,128)S(1)} %get-tuple-element.36), channel_id=1, source_target_pairs={{0,1},{1,2},{2,3},{3,4},{4,5},{5,6},{6,7},{7,8},{8,9},{9,10},{10,1... | collective-permute-start | bytes 1228808 | tf_op jit(solution)/shard_map/ppermute | solution.py:25
  41.5 7.2 %collective-permute-start.3 = (f32[2,50,1,1024]{3,2,1,0:T(1,128)S(1)}, f32[2,50,1,1024]{3,2,1,0:T(1,128)S(1)}, u32[]{:S(2)}, u32[]{:S(2)}) collective-permute-start(f32[2,50,1,1024]{3,2,1,0:T(1,128)S(1)} %get-tuple-element.37), channel_id=1, source_target_pairs={{1,0},{2,1},{3,2},{4,3},{5,4},{6,5},{7,6},{8,7},{9,8},{10,9},{11,1... | collective-permute-start | bytes 1228808 | tf_op jit(solution)/shard_map/ppermute | solution.py:28
  52.2 5.8 %collective-permute-start.5 = (f32[2,1,1024]{2,1,0:T(1,128)S(1)}, f32[2,1,1024]{2,1,0:T(1,128)S(1)}, u32[]{:S(2)}, u32[]{:S(2)}) collective-permute-start(f32[2,1,1024]{2,1,0:T(1,128)S(1)} %get-tuple-element.42), channel_id=1, source_target_pairs={{0,1},{1,2},{2,3},{3,4},{4,5},{5,6},{6,7},{7,8},{8,9},{9,10},{10,1... | collective-permute-start | bytes 24584 | tf_op jit(solution)/shard_map/ppermute | solution.py:25
  56.3 1.8 collective-permute-start.4
  122.3 5.8 %collective-permute-start.7 = (f32[2,1,1024]{2,1,0:T(1,128)S(1)}, f32[2,1,1024]{2,1,0:T(1,128)S(1)}, u32[]{:S(2)}, u32[]{:S(2)}) collective-permute-start(f32[2,1,1024]{2,1,0:T(1,128)S(1)} %get-tuple-element.40), channel_id=1, source_target_pairs={{0,1},{1,2},{2,3},{3,4},{4,5},{5,6},{6,7},{7,8},{8,9},{9,10},{10,1... | collective-permute-start | bytes 24584 | tf_op jit(solution)/shard_map/ppermute | solution.py:25
  122.4 5.8 %collective-permute-start.6 = (f32[2,1,1024]{2,1,0:T(1,128)S(1)}, f32[2,1,1024]{2,1,0:T(1,128)S(1)}, u32[]{:S(2)}, u32[]{:S(2)}) collective-permute-start(f32[2,1,1024]{2,1,0:T(1,128)S(1)} %get-tuple-element.41), channel_id=1, source_target_pairs={{1,0},{2,1},{3,2},{4,3},{5,4},{6,5},{7,6},{8,7},{9,8},{10,9},{11,1... | collective-permute-start | bytes 24584 | tf_op jit(solution)/shard_map/ppermute | solution.py:28
  192.4 5.8 %collective-permute-start.9 = (f32[2,1,1024]{2,1,0:T(1,128)S(1)}, f32[2,1,1024]{2,1,0:T(1,128)S(1)}, u32[]{:S(2)}, u32[]{:S(2)}) collective-permute-start(f32[2,1,1024]{2,1,0:T(1,128)S(1)} %get-tuple-element.38), channel_id=1, source_target_pairs={{0,1},{1,2},{2,3},{3,4},{4,5},{5,6},{6,7},{7,8},{8,9},{9,10},{10,1... | collective-permute-start | bytes 24584 | tf_op jit(solution)/shard_map/ppermute | solution.py:25
  192.4 5.8 %collective-permute-start.8 = (f32[2,1,1024]{2,1,0:T(1,128)S(1)}, f32[2,1,1024]{2,1,0:T(1,128)S(1)}, u32[]{:S(2)}, u32[]{:S(2)}) collective-permute-start(f32[2,1,1024]{2,1,0:T(1,128)S(1)} %get-tuple-element.39), channel_id=1, source_target_pairs={{1,0},{2,1},{3,2},{4,3},{5,4},{6,5},{7,6},{8,7},{9,8},{10,9},{11,1... | collective-permute-start | bytes 24584 | tf_op jit(solution)/shard_map/ppermute | solution.py:28
